TPU v7x, 32 devices: a whole 2x2x4 slice. The times are simulated.
32 devices in a mesh: seq: 8 (over z, core), grp: 2 (over y), dp: 2 (over x).
Axes of the slice: x: 2, y: 2, z: 4, core: 2. Of those that a mesh axis runs over, the one named last changes fastest.
Arguments:
- clips: bfloat16 [2, 1024, 1408], P('dp', 'seq'), may hold values from -6 to 6
- context: int32 [2, 1024], P('dp', 'seq'), may hold values from 0 to 1, as said below
- predict_index: int32 [2, 1536], P('dp', 'seq'), may hold values from -1 to 1023, as said below
- target_qkv: bfloat16 [3, 1408, 1408], P(None, 'dp', 'grp'), may hold values from -8 to 8
- target_out: bfloat16 [1408, 1408], P('grp'), may hold values from -0.15625 to 0.15625
- student_qkv: bfloat16 [3, 1408, 1408], P(None, 'dp', 'grp'), may hold values from -8 to 8
- student_out: bfloat16 [1408, 1408], P('grp', 'dp'), may hold values from -0.15625 to 0.15625
- mask_token: float32 [1408], replicated, may hold values from -4 to 4
Outputs:
- out_grad: float32 [1408, 1408], P('grp', 'dp')
- target_blend: float32 [1408, 1408], P('grp')
Inputs may be any that keep to these rules, and one draw needn't show every extreme that they name: In every aligned block of 128 tokens of a clip exactly 32 tokens have context 1 and the others 0. `predict_index`: each device's 192 slots name distinct target positions (context 0) of its clip, followed by -1 in the unused slots; different devices' lists may name the same position. In every clip one list is full.
All inputs are finite; a program needn't handle non-finite values.
Results may differ from a plain program's by a relative error of at most 0.014.
Values may be sent and summed in bfloat16 or wider, within the bound.
A program may use at most 128 MiB of HBM per device.

v0:
```python
import math
import jax
import jax.numpy as jnp
from jax import lax
from jax.sharding import PartitionSpec as P

HEAD_DIM = 88
CTX_DEV = 32
EPSILON = 1e-06
MOMENTUM = 0.99


def layer_norm(values):
    center = values - jnp.mean(values, axis=-1, keepdims=True)
    factor = lax.rsqrt(jnp.mean(center * center, axis=-1, keepdims=True) + EPSILON)
    return (center * factor, factor)


def position_table(places, width):
    half_width = width // 2
    spacing = jnp.exp(jnp.arange(half_width, dtype=jnp.float32) * (-math.log(10000.0) / half_width))
    angles = places.astype(jnp.float32)[:, None] * spacing[None, :]
    return jnp.concatenate([jnp.sin(angles), jnp.cos(angles)], axis=1)


def to_heads(queries):
    head_count = queries.shape[1] // HEAD_DIM
    return queries.reshape(queries.shape[0], head_count, HEAD_DIM).transpose(1, 0, 2)


def empty_state(head_count, row_count):
    peaks = jnp.full((head_count, row_count), -1e30, jnp.float32)
    totals = jnp.zeros((head_count, row_count), jnp.float32)
    summed = jnp.zeros((head_count, row_count, HEAD_DIM), jnp.float32)
    return (peaks, totals, summed)


def from_heads(running):
    peaks, totals, summed = running
    mixed = summed / totals[:, :, None]
    head_count, row_count, unused = mixed.shape
    return mixed.transpose(1, 0, 2).reshape(row_count, head_count * HEAD_DIM).astype(jnp.bfloat16)


def attend_shard(running, shard_rows, query_heads):
    peaks, totals, summed = running
    key_rows, value_rows = shard_rows
    length = key_rows.shape[0]
    head_count = query_heads.shape[0]
    key_heads = key_rows.reshape(length, head_count, HEAD_DIM)
    value_heads = value_rows.reshape(length, head_count, HEAD_DIM)
    factor = HEAD_DIM ** (-0.5)
    scores = (
        jnp.einsum("hqd,khd->hqk", query_heads, key_heads, preferred_element_type=jnp.float32)
        * factor
    )
    raised = jnp.maximum(peaks, jnp.max(scores, axis=2))
    shifted = jnp.exp(scores - raised[:, :, None])
    totals = jnp.sum(shifted, axis=2)
    summed = jnp.einsum(
        "hqk,khd->hqd",
        shifted.astype(jnp.bfloat16),
        value_heads,
        preferred_element_type=jnp.float32,
    )
    return (raised, totals, summed)


def body(
    clips, context, predict_index, target_qkv, target_out, student_qkv, student_out, mask_token
):
    tokens = clips[0]
    keep_flags = context[0]
    listed = predict_index[0]
    row_count, width = tokens.shape
    half_width = target_qkv.shape[2]
    head_count = half_width // HEAD_DIM
    normed = layer_norm(tokens.astype(jnp.float32))[0].astype(jnp.bfloat16)
    projected = jnp.einsum(
        "nr,krc->knc",
        normed,
        lax.all_gather(target_qkv, "dp", axis=1, tiled=True),
        preferred_element_type=jnp.float32,
    )
    projected = projected.astype(jnp.bfloat16)
    target_state = attend_shard(
        empty_state(head_count, row_count),
        (
            lax.all_gather(projected[1], "seq", axis=0, tiled=True),
            lax.all_gather(projected[2], "seq", axis=0, tiled=True),
        ),
        query_heads=to_heads(projected[0]),
    )
    target_mixed = from_heads(target_state)
    target_part = jnp.dot(target_mixed, target_out, preferred_element_type=jnp.float32)
    target_sum = lax.psum(target_part.astype(jnp.bfloat16), "grp").astype(jnp.float32)
    features = layer_norm(tokens.astype(jnp.float32) + target_sum)[0].astype(jnp.bfloat16)
    first_row = lax.axis_index("seq") * row_count
    every_list = lax.all_gather(listed, "seq", axis=0, tiled=True)
    places = first_row + jnp.arange(row_count, dtype=jnp.int32)
    usable = jnp.sum((every_list[None, :] == places[:, None]).astype(jnp.float32), axis=1)
    slot_count = places.shape[0]
    is_context = keep_flags == 1
    context_order = jnp.cumsum(is_context.astype(jnp.int32)) - 1
    selector = (
        (context_order[None, :] == jnp.arange(CTX_DEV, dtype=jnp.int32)[:, None])
        & is_context[None, :]
    ).astype(jnp.bfloat16)
    context_rows = jnp.dot(selector, normed, preferred_element_type=jnp.float32).astype(
        jnp.bfloat16
    )
    seeds = mask_token[None, :] + position_table(jnp.maximum(places, 0), width)
    seed_normed = layer_norm(seeds)[0].astype(jnp.bfloat16)
    shard_rows = lax.all_gather(student_qkv, "dp", axis=1, tiled=True)
    query_total = jnp.dot(seed_normed, shard_rows[0], preferred_element_type=jnp.float32)
    pair_total = jnp.einsum(
        "nr,krc->knc", context_rows, shard_rows[1:], preferred_element_type=jnp.float32
    )
    student_pairs = pair_total
    student_pairs = student_pairs.astype(jnp.bfloat16)
    student_state = attend_shard(
        empty_state(head_count, slot_count),
        (
            lax.all_gather(student_pairs[0], "seq", axis=0, tiled=True),
            lax.all_gather(student_pairs[1], "seq", axis=0, tiled=True),
        ),
        query_heads=to_heads(query_total.astype(jnp.bfloat16)),
    )
    student_mixed = from_heads(student_state)
    relaid = lax.all_gather(student_out, "dp", axis=1, tiled=True)
    student_part = jnp.dot(student_mixed, relaid, preferred_element_type=jnp.float32)
    student_sum = lax.psum(student_part.astype(jnp.bfloat16), "grp").astype(jnp.float32)
    predicted, factor = layer_norm(seeds + student_sum)
    wanted = features.astype(jnp.float32)
    slope = jnp.clip(predicted - wanted, -1.0, 1.0) * usable[:, None]
    back_grad = (
        slope
        - jnp.mean(slope, axis=1, keepdims=True)
        - predicted * jnp.mean(slope * predicted, axis=1, keepdims=True)
    ) * factor
    local_grad = jnp.dot(
        student_mixed.astype(jnp.float32).T, back_grad, precision=lax.Precision.HIGHEST
    )
    column_grad = lax.psum_scatter(
        local_grad.astype(jnp.bfloat16), "dp", scatter_dimension=1, tiled=True
    )
    out_grad = lax.psum(column_grad, "seq").astype(jnp.float32)
    target_blend = MOMENTUM * target_out.astype(jnp.float32) + (1.0 - MOMENTUM) * relaid.astype(
        jnp.float32
    )
    return (out_grad, target_blend)


def solution(mesh):
    in_specs = (
        P("dp", "seq", None),
        P("dp", "seq"),
        P("dp", "seq"),
        P(None, "dp", "grp"),
        P("grp", None),
        P(None, "dp", "grp"),
        P("grp", "dp"),
        P(),
    )
    out_specs = (P("grp", "dp"), P("grp", None))
    return jax.shard_map(body, mesh=mesh, in_specs=in_specs, out_specs=out_specs, check_vma=False)
```

profile of v0, /device:TPU:0, one launch (start us, length us, event | category | flops | bytes accessed | tf_op | source)
XLA Modules:
  0.0 480.1 jit_solution(4295476264770077709)
XLA Ops:
  7.2 0.0 all-gather.15.cloned.1.call-start
  7.2 6.9 %copy.48 = bf16[3,704,704]{2,0,1:T(4,128)(2,1)} copy(bf16[3,704,704]{2,1,0:T(8,128)(2,1)} %param.11) | data formatting | bytes 5947392 | tf_op args[3]
  14.2 0.0 all-gather.11.cloned.1.call-start
  14.2 4.8 %copy.41 = bf16[3,704,704]{2,0,1:T(4,128)(2,1)} copy(bf16[3,704,704]{2,1,0:T(8,128)(2,1)S(1)} %copy-done.5) | data formatting | bytes 5947392 | tf_op args[5]
  19.1 0.0 all-gather.13.cloned.1.call-start
  19.1 1.2 copy-done.6
  20.3 1.5 copy.47
  21.8 0.0 all-gather.17.cloned.1.call-start
  21.8 0.1 convert_reduce_fusion
  21.9 0.2 fusion.45
  22.2 104.2 %all-gather.15.cloned.1.call-done = bf16[3,1408,704]{2,0,1:T(4,128)(2,1)} async-done(((bf16[3,704,704]{2,0,1:T(4,128)(2,1)}), bf16[3,1408,704]{2,0,1:T(4,128)(2,1)}) %all-gather.15.cloned.1.call-update) | async-done | bytes 5947408 | tf_op jit(solution)/shard_map/all_gather | solution.py:82
  126.4 6.0 %fusion.16 = bf16[3,128,704]{1,2,0:T(8,128)(2,1)S(1)} fusion(bf16[3,1408,704]{2,0,1:T(4,128)(2,1)} %all-gather.15.cloned.1.call-done, bf16[1,128,1408]{2,1,0:T(8,128)(2,1)S(1)} %copy-done.1, f32[128]{0:T(128)S(1)} %add_rsqrt_fusion.2, f32[128]{0:T(128)S(1)} %broadcast_multiply_fusion.4), kind=kOutput, calls=%fused_computation.21 | convolution fusion | flops 762257408 | bytes 6849536 | tf_op jit(solution)/shard_map/nr,krc->knc/dot_general | solution.py:79
  132.4 0.8 fusion.83
  133.2 0.2 all-gather.19.cloned.1.call-start
  133.5 0.1 copy.43
  133.6 0.2 reduce-window.8
  133.8 0.1 add_reduce_fusion
  133.9 1.4 multiply_sine_fusion
  135.4 0.2 fusion.66
  135.6 0.3 multiply_reduce_fusion.4
  135.9 101.4 %all-gather.11.cloned.1.call-done = bf16[3,1408,704]{2,0,1:T(4,128)(2,1)} async-done(((bf16[3,704,704]{2,0,1:T(4,128)(2,1)}), bf16[3,1408,704]{2,0,1:T(4,128)(2,1)}) %all-gather.11.cloned.1.call-update) | async-done | bytes 5947408 | tf_op jit(solution)/shard_map/all_gather | solution.py:114
  237.3 7.6 %slice.29 = bf16[2,1408,704]{2,0,1:T(2,128)(2,1)} slice(bf16[3,1408,704]{2,0,1:T(4,128)(2,1)} %all-gather.11.cloned.1.call-done), slice={[1:3], [0:1408], [0:704]} | slice | bytes 7929856 | tf_op jit(solution)/shard_map/slice | solution.py:117
  244.9 3.7 fusion.30
  248.6 0.6 fusion.84
  249.3 14.5 %all-gather.1 = bf16[1,256,704]{2,1,0:T(8,128)(2,1)S(1)} all-gather(bf16[1,32,704]{2,1,0:T(8,128)(2,1)S(1)} %get-tuple-element.19), channel_id=3, replica_groups=mesh['seq'=8,'grp'=2,'dp'=2] {'seq'}, dimensions={1}, use_global_device_ids=true | all-gather | bytes 405504 | tf_op jit(solution)/shard_map/all_gather | solution.py:125
  263.7 0.9 copy.46
  264.7 7.1 %slice.28 = bf16[1,1408,704]{2,0,1:T(2,128)(2,1)} slice(bf16[3,1408,704]{2,0,1:T(4,128)(2,1)} %all-gather.11.cloned.1.call-done), slice={[0:1], [0:1408], [0:704]} | slice | bytes 3964928 | tf_op jit(solution)/shard_map/slice | solution.py:115
  271.7 12.0 %copy.54 = bf16[1,1408,704]{1,2,0:T(8,128)(2,1)S(1)} copy(bf16[1,1408,704]{2,0,1:T(2,128)(2,1)} %slice.28) | data formatting | bytes 3964928
  283.8 0.0 all-gather.19.cloned.1.call-update
  283.8 0.0 all-reduce.7.cloned.1.call-start
  283.8 16.5 %all-gather = bf16[1,256,704]{2,1,0:T(8,128)(2,1)S(1)} all-gather(bf16[1,32,704]{2,1,0:T(8,128)(2,1)} %get-tuple-element.18), channel_id=2, replica_groups=mesh['seq'=8,'grp'=2,'dp'=2] {'seq'}, dimensions={1}, use_global_device_ids=true | all-gather | bytes 405504 | tf_op jit(solution)/shard_map/all_gather | solution.py:124
  300.3 0.9 copy.45
  301.2 0.8 fusion.23
  302.0 1.4 fusion.85
  303.5 0.4 fusion.39
  303.9 0.4 fusion.26
  304.3 0.0 all-gather.13.cloned.1.call-done
  304.3 3.2 convolution_convert_fusion.2
  307.5 2.2 multiply_reduce_fusion
  309.7 1.9 copy-done
  311.6 0.9 fusion.4
  312.5 18.5 %all-gather.19.cloned.1.call-done = bf16[1,1024,704]{1,2,0:T(8,128)(2,1)} async-done(((bf16[1,128,704]{1,2,0:T(8,128)(2,1)}), bf16[1,1024,704]{1,2,0:T(8,128)(2,1)}) %all-gather.19.cloned.1.call-update) | async-done | bytes 1441808 | tf_op jit(solution)/shard_map/all_gather | solution.py:90
  331.0 3.6 fusion.36
  334.7 1.2 convolution_convert_fusion.1
  336.0 0.0 reduce-scatter.4.cloned.1.call-start
  336.0 0.6 dynamic-slice
  337.3 0.3 dynamic-update-slice
  337.6 7.6 %all-reduce = s32[1536]{0:T(1024)S(1)} all-reduce(s32[1536]{0:T(1024)S(1)} %dynamic-update-slice), channel_id=6, replica_groups=mesh['seq'=8,'grp'=2,'dp'=2] {'seq'}, use_global_device_ids=true, to_apply=%add | all-reduce | flops 1536 | bytes 12288
  345.2 0.2 convert_reduce_fusion.1
  345.4 22.1 %all-reduce.7.cloned.1.call-done = (bf16[128,1408]{1,0:T(8,128)(2,1)}, bf16[128,1408]{1,0:T(8,128)(2,1)}) async-done(((bf16[128,1408]{1,0:T(8,128)(2,1)}, bf16[128,1408]{1,0:T(8,128)(2,1)}), (bf16[128,1408]{1,0:T(8,128)(2,1)}, bf16[128,1408]{1,0:T(8,128)(2,1)})) %all-reduce.7.cloned.1.call-update) | async-done | bytes 720912 | tf_op jit(solution)/shard_map/psum | solution.py:96
  367.6 1.2 fusion.53
  368.8 1.4 fusion.82
  370.3 0.2 multiply_reduce_fusion.3
  370.5 0.5 fusion.51
  371.0 2.0 convolution_convert_fusion
  373.0 2.5 copy.52
  375.5 0.0 all-reduce.5.cloned.1.call-start
  375.6 4.1 copy.50
  379.7 28.6 %reduce-scatter.4.cloned.1.call-done = bf16[704,704]{1,0:T(8,128)(2,1)} async-done(((bf16[1408,704]{1,0:T(8,128)(2,1)}), bf16[704,704]{1,0:T(8,128)(2,1)}) %reduce-scatter.4.cloned.1.call-update) | async-done | bytes 991248
  408.3 2.3 copy.53
  410.7 4.3 multiply_add_fusion
  415.0 5.6 %copy.51 = f32[704,1408]{1,0:T(8,128)} copy(f32[704,1408]{0,1:T(8,128)} %multiply_add_fusion) | data formatting | bytes 7929856
  420.6 49.9 %all-reduce.5.cloned.1.call-done = bf16[704,704]{1,0:T(8,128)(2,1)} async-done(((bf16[704,704]{1,0:T(8,128)(2,1)}), bf16[704,704]{1,0:T(8,128)(2,1)}) %all-reduce.5.cloned.1.call-update) | async-done | bytes 991248 | tf_op jit(solution)/shard_map/psum | solution.py:147
  470.5 2.7 convert_element_type.121
  (49 shorter events, 0.3 us)
Async XLA Ops:
  7.2 7.1 %copy-start.5 = (bf16[3,704,704]{2,1,0:T(8,128)(2,1)S(1)}, bf16[3,704,704]{2,1,0:T(8,128)(2,1)}, u32[]{:S(2)}) copy-start(bf16[3,704,704]{2,1,0:T(8,128)(2,1)} %param.13) | copy-start | bytes 8921092
  7.2 119.2 %all-gather.15.cloned.1.call-start = ((), (), s32[]{:S(2)}) async-start(), calls=%async_computation.3 | async-start | bytes 12976128 | tf_op jit(solution)/shard_map/all_gather | solution.py:82
  14.2 223.2 %all-gather.11.cloned.1.call-start = ((), (), s32[]{:S(2)}) async-start(), calls=%async_computation.1 | async-start | bytes 12976128 | tf_op jit(solution)/shard_map/all_gather | solution.py:114
  19.0 1.2 copy-start.6
  19.0 2.8 copy-start.1
  19.1 285.2 %all-gather.13.cloned.1.call-start = ((), (), s32[]{:S(2)}) async-start(), calls=%async_computation.2 | async-start | bytes 3244032 | tf_op jit(solution)/shard_map/all_gather | solution.py:130
  21.8 285.7 %all-gather.17.cloned.1.call-start = ((), (), s32[]{:S(2)}) async-start(), calls=%async_computation.5 | async-start | bytes 1622016 | tf_op jit(solution)/shard_map/all_gather | solution.py:89
  22.2 111.3 %copy-start.11 = (s32[1,128]{1,0:T(1,128)S(1)}, s32[1,128]{1,0:T(1,128)}, u32[]{:S(2)}) copy-start(s32[1,128]{1,0:T(1,128)} %param.9) | copy-start | bytes 1540
  22.2 113.1 %copy-start.9 = (f32[1408]{0:T(1024)S(1)}, f32[1408]{0:T(1024)}, u32[]{:S(2)}) copy-start(f32[1408]{0:T(1024)} %param.15) | copy-start | bytes 16900
  133.2 197.8 %all-gather.19.cloned.1.call-start = ((), (), s32[]{:S(2)}) async-start(), calls=%async_computation.6 | async-start | bytes 1622016 | tf_op jit(solution)/shard_map/all_gather | solution.py:90
  283.8 83.8 %all-reduce.7.cloned.1.call-start = ((), (), s32[]{:S(2)}) async-start(), calls=%async_computation.8 | async-start | bytes 1441792 | tf_op jit(solution)/shard_map/psum | solution.py:96
  301.2 2.6 copy-start.8
  302.0 5.5 %copy-start.7 = (bf16[1,128,704]{1,2,0:T(8,128)(2,1)S(1)}, bf16[1,128,704]{1,2,0:T(8,128)(2,1)}, u32[]{:S(2)}) copy-start(bf16[1,128,704]{1,2,0:T(8,128)(2,1)} %get-tuple-element.17) | copy-start | bytes 540676
  309.7 1.9 copy-start
  312.5 22.2 %copy-start.3 = (bf16[704,1408]{1,0:T(8,128)(2,1)S(1)}, bf16[704,1408]{1,0:T(8,128)(2,1)}, u32[]{:S(2)}) copy-start(bf16[704,1408]{1,0:T(8,128)(2,1)} %param.12) | copy-start | bytes 5947396
  331.0 5.0 %copy-start.12 = (u32[32]{0:T(128)S(1)}, u32[32]{0:T(128)}, u32[]{:S(2)}) copy-start(u32[32]{0:T(128)} %constant.55) | copy-start | bytes 388
  331.0 6.3 %copy-start.10 = (s32[1,192]{1,0:T(1,128)S(1)}, s32[1,192]{1,0:T(1,128)}, u32[]{:S(2)}) copy-start(s32[1,192]{1,0:T(1,128)} %param.10) | copy-start | bytes 2308
  336.0 72.4 %reduce-scatter.4.cloned.1.call-start = ((), (), s32[]{:S(2)}) async-start(), calls=%async_computation.7 | async-start | bytes 3244032
  367.6 2.9 copy-start.4
  375.5 35.1 %copy-start.2 = (bf16[704,1408]{0,1:T(8,128)(2,1)S(1)}, bf16[704,1408]{0,1:T(8,128)(2,1)}, u32[]{:S(2)}) copy-start(bf16[704,1408]{0,1:T(8,128)(2,1)} %all-gather.13.cloned.1.call-done) | copy-start | bytes 5947396
  375.5 95.0 %all-reduce.5.cloned.1.call-start = ((), (), s32[]{:S(2)}) async-start(), calls=%async_computation.4 | async-start | bytes 2162688 | tf_op jit(solution)/shard_map/psum | solution.py:147
Sparse Core Ops, SparseCore 0:
  14.3 112.0 all-gather.14
  128.0 109.3 all-gather.10
  239.5 33.8 all-gather.12
  274.8 28.2 all-gather.16
  304.5 26.4 all-gather.18
  336.1 31.4 all-reduce.6
  375.7 32.6 reduce-scatter.3
  411.2 59.2 all-reduce.4
where the time goes:
time: 481 us; the launch traced here: 480 us
  waiting for transfers between devices  325 us (68%)
  local copies, waits for them, and re-layouts  61.8 us (13%)
  blocking collectives  38.6 us (8%)
  matrix products  24.5 us (5%)
  between operations  15.1 us (3%)
  other arithmetic  14.7 us (3%)
    all_gather x1, waiting for transfers between devices, body(): lax.all_gather(target_qkv, 'dp', axis=1, tiled=True)  104 us
    all_gather x1, waiting for transfers between devices, body(): shard_rows = lax.all_gather(student_qkv, 'dp', axis=1, tiled=True)  101 us
    psum x1, waiting for transfers between devices, body(): out_grad = lax.psum(column_grad, 'seq').astype(jnp.float32)  49.9 us
    unnamed x37, local copies, waits for them, and re-layouts  43.8 us
    unnamed x9, waiting for transfers between devices  28.7 us
    psum x1, waiting for transfers between devices, body(): lax.psum(target_part.astype(jnp.bfloat16), 'grp').astype(jnp.float32)  22.1 us
    all_gather x1, waiting for transfers between devices, body(): lax.all_gather(projected[2], 'seq', axis=0, tiled=True)  18.5 us
    all_gather x1, blocking collectives, body(): lax.all_gather(student_pairs[0], 'seq', axis=0, tiled=True)  16.5 us
  transfers between devices with their start and end apart: 8, of which 6 were waited for; matrix products, arithmetic and copies ran while one was open for 15% of the time, Pallas kernels for 0%

commit v1 on v0

--- a/solution.py
+++ b/solution.py
@@ -1,3 +1,4 @@
+import functools
 import math
 import jax
 import jax.numpy as jnp
@@ -8,6 +9,14 @@
 CTX_DEV = 32
 EPSILON = 1e-06
 MOMENTUM = 0.99
+
+
+def review_surface_on(tile_in, a_name, on_dim):
+    work_now = lax.all_gather(tile_in, a_name)
+    return jnp.concatenate(work_now, axis=on_dim)
+
+
+_process_classes = functools.partial(review_surface_on, a_name="dp", on_dim=1)
 
 
 def layer_norm(values):
@@ -77,10 +86,7 @@
     head_count = half_width // HEAD_DIM
     normed = layer_norm(tokens.astype(jnp.float32))[0].astype(jnp.bfloat16)
     projected = jnp.einsum(
-        "nr,krc->knc",
-        normed,
-        lax.all_gather(target_qkv, "dp", axis=1, tiled=True),
-        preferred_element_type=jnp.float32,
+        "nr,krc->knc", normed, _process_classes(target_qkv), preferred_element_type=jnp.float32
     )
     projected = projected.astype(jnp.bfloat16)
     target_state = attend_shard(

time: 481 us -> 450 us (0.936)
  waiting for transfers between devices: 325 us -> 268 us
  local copies, waits for them, and re-layouts: 61.8 us -> 88.8 us
    all_gather x1, waiting for transfers between devices: 101 us -> 70.4 us  [body(): shard_rows = lax.all_gather(student_qkv, 'dp', axis=1, tiled=True)]
    all_gather x1, waiting for transfers between devices: 104 us -> 77.7 us  [review_surface_on(): work_now = lax.all_gather(tile_in, a_name)]
    all_gather x0 -> x1, local copies, waits for them, and re-layouts: none -> 18.4 us  [review_surface_on(): work_now = lax.all_gather(tile_in, a_name)]
    reshape x0 -> x1, local copies, waits for them, and re-layouts: none -> 14.3 us  [review_surface_on(): return jnp.concatenate(work_now, axis=on_dim)]
    unnamed x37 -> x36, local copies, waits for them, and re-layouts: 43.8 us -> 38.1 us
  transfers between devices with their start and end apart: 8 -> 8, of which waited for: 6 -> 6; matrix products, arithmetic and copies ran while one was open for 15% -> 23% of each run, Pallas kernels for 0% -> 0%
where the time goes in v1:
time: 450 us; the launch traced here: 449 us
  waiting for transfers between devices  268 us (60%)
  local copies, waits for them, and re-layouts  88.8 us (20%)
  blocking collectives  38.7 us (9%)
  matrix products  23 us (5%)
  between operations  15 us (3%)
  other arithmetic  14.7 us (3%)
    all_gather x1, waiting for transfers between devices, review_surface_on(): work_now = lax.all_gather(tile_in, a_name)  77.7 us
    all_gather x1, waiting for transfers between devices, body(): shard_rows = lax.all_gather(student_qkv, 'dp', axis=1, tiled=True)  70.4 us
    psum x1, waiting for transfers between devices, body(): out_grad = lax.psum(column_grad, 'seq').astype(jnp.float32)  49.9 us
    unnamed x36, local copies, waits for them, and re-layouts  38.1 us
    unnamed x9, waiting for transfers between devices  29.4 us
    psum x1, waiting for transfers between devices, body(): lax.psum(target_part.astype(jnp.bfloat16), 'grp').astype(jnp.float32)  22.1 us
    all_gather x1, waiting for transfers between devices, body(): lax.all_gather(projected[2], 'seq', axis=0, tiled=True)  18.5 us
    all_gather x1, local copies, waits for them, and re-layouts, review_surface_on(): work_now = lax.all_gather(tile_in, a_name)  18.4 us
  transfers between devices with their start and end apart: 8, of which 6 were waited for; matrix products, arithmetic and copies ran while one was open for 23% of the time, Pallas kernels for 0%

profile of v1, /device:TPU:0, one launch (start us, length us, event | category | flops | bytes accessed | tf_op | source)
XLA Modules:
  0.0 448.7 jit_solution(6439592363940196900)
XLA Ops:
  7.2 0.7 all-gather.16.cloned.1.call-update
  7.9 0.0 all-gather.12.cloned.1.call-start
  8.0 1.1 copy-done.5
  9.1 4.8 %copy.39 = bf16[3,704,704]{2,0,1:T(4,128)(2,1)} copy(bf16[3,704,704]{2,1,0:T(8,128)(2,1)S(1)} %copy-done.5) | data formatting | bytes 5947392 | tf_op args[5]
  14.0 0.0 all-gather.14.cloned.1.call-start
  14.0 1.2 copy-done.6
  15.2 1.5 copy.45
  16.7 0.0 all-gather.18.cloned.1.call-start
  16.7 0.1 convert_reduce_fusion
  16.9 0.2 fusion.38
  17.1 77.7 %all-gather.16.cloned.1.call-done = bf16[6,704,704]{2,1,0:T(8,128)(2,1)} async-done(((bf16[3,704,704]{2,1,0:T(8,128)(2,1)}), bf16[6,704,704]{2,1,0:T(8,128)(2,1)}) %all-gather.16.cloned.1.call-update) | async-done | bytes 5947408 | tf_op jit(solution)/shard_map/all_gather | solution.py:15
  94.8 18.4 %copy.46 = bf16[2,3,704,704]{2,0,3,1:T(2,128)(2,1)} copy(bf16[2,3,704,704]{3,2,1,0:T(8,128)(2,1)} %bitcast.94) | data formatting | bytes 11894784 | tf_op jit(solution)/shard_map/all_gather | solution.py:15
  113.3 14.3 %reshape.161 = bf16[3,1408,704]{1,2,0:T(8,128)(2,1)} reshape(bf16[3,2,704,704]{2,1,3,0:T(2,128)(2,1)} %bitcast.92) | data formatting | bytes 11894784 | tf_op jit(solution)/shard_map/reshape | solution.py:16
  127.6 4.5 %fusion.11 = bf16[3,128,704]{1,2,0:T(8,128)(2,1)S(1)} fusion(bf16[3,1408,704]{1,2,0:T(8,128)(2,1)} %reshape.161, bf16[1,128,1408]{2,1,0:T(8,128)(2,1)S(1)} %copy-done.1, f32[128]{0:T(128)S(1)} %add_rsqrt_fusion.2, f32[128]{0:T(128)S(1)} %broadcast_multiply_fusion.4), kind=kOutput, calls=%fused_computation.19 | convolution fusion | flops 762257408 | bytes 6849536 | tf_op jit(solution)/shard_map/nr,krc->knc/dot_general | solution.py:88
  132.1 0.8 fusion.84
  132.9 0.0 all-gather.20.cloned.1.call-start
  133.0 0.1 copy.41
  133.1 0.2 reduce-window.8
  133.3 0.1 add_reduce_fusion
  133.4 1.4 multiply_sine_fusion
  134.8 0.2 fusion.70
  135.1 0.3 multiply_reduce_fusion.4
  135.4 70.4 %all-gather.12.cloned.1.call-done = bf16[3,1408,704]{2,0,1:T(4,128)(2,1)} async-done(((bf16[3,704,704]{2,0,1:T(4,128)(2,1)}), bf16[3,1408,704]{2,0,1:T(4,128)(2,1)}) %all-gather.12.cloned.1.call-update) | async-done | bytes 5947408 | tf_op jit(solution)/shard_map/all_gather | solution.py:120
  205.8 7.6 %slice.29 = bf16[2,1408,704]{2,0,1:T(2,128)(2,1)} slice(bf16[3,1408,704]{2,0,1:T(4,128)(2,1)} %all-gather.12.cloned.1.call-done), slice={[1:3], [0:1408], [0:704]} | slice | bytes 7929856 | tf_op jit(solution)/shard_map/slice | solution.py:123
  213.4 3.7 fusion.23
  217.1 0.6 fusion.85
  217.7 14.6 %all-gather.1 = bf16[1,256,704]{2,1,0:T(8,128)(2,1)S(1)} all-gather(bf16[1,32,704]{2,1,0:T(8,128)(2,1)S(1)} %get-tuple-element.19), channel_id=3, replica_groups=mesh['seq'=8,'grp'=2,'dp'=2] {'seq'}, dimensions={1}, use_global_device_ids=true | all-gather | bytes 405504 | tf_op jit(solution)/shard_map/all_gather | solution.py:131
  232.4 0.9 copy.44
  233.3 7.1 %slice.28 = bf16[1,1408,704]{2,0,1:T(2,128)(2,1)} slice(bf16[3,1408,704]{2,0,1:T(4,128)(2,1)} %all-gather.12.cloned.1.call-done), slice={[0:1], [0:1408], [0:704]} | slice | bytes 3964928 | tf_op jit(solution)/shard_map/slice | solution.py:121
  240.3 12.0 %copy.51 = bf16[1,1408,704]{1,2,0:T(8,128)(2,1)S(1)} copy(bf16[1,1408,704]{2,0,1:T(2,128)(2,1)} %slice.28) | data formatting | bytes 3964928
  252.4 0.0 all-reduce.7.cloned.1.call-start
  252.4 16.4 %all-gather = bf16[1,256,704]{2,1,0:T(8,128)(2,1)S(1)} all-gather(bf16[1,32,704]{2,1,0:T(8,128)(2,1)} %get-tuple-element.18), channel_id=2, replica_groups=mesh['seq'=8,'grp'=2,'dp'=2] {'seq'}, dimensions={1}, use_global_device_ids=true | all-gather | bytes 405504 | tf_op jit(solution)/shard_map/all_gather | solution.py:130
  268.8 0.9 copy.43
  269.7 0.8 fusion.16
  270.5 1.4 fusion.86
  272.0 0.4 fusion.32
  272.4 0.4 fusion.19
  272.8 3.2 convolution_convert_fusion.2
  276.0 2.2 multiply_reduce_fusion
  278.2 1.9 copy-done
  280.1 0.9 fusion.2
  281.0 18.5 %all-gather.20.cloned.1.call-done = bf16[1,1024,704]{1,2,0:T(8,128)(2,1)} async-done(((bf16[1,128,704]{1,2,0:T(8,128)(2,1)}), bf16[1,1024,704]{1,2,0:T(8,128)(2,1)}) %all-gather.20.cloned.1.call-update) | async-done | bytes 1441808 | tf_op jit(solution)/shard_map/all_gather | solution.py:96
  299.6 3.6 fusion.29
  303.2 1.2 convolution_convert_fusion.1
  304.5 0.0 reduce-scatter.4.cloned.1.call-start
  304.6 0.6 dynamic-slice
  305.8 0.3 dynamic-update-slice
  306.1 7.6 %all-reduce = s32[1536]{0:T(1024)S(1)} all-reduce(s32[1536]{0:T(1024)S(1)} %dynamic-update-slice), channel_id=7, replica_groups=mesh['seq'=8,'grp'=2,'dp'=2] {'seq'}, use_global_device_ids=true, to_apply=%add | all-reduce | flops 1536 | bytes 12288
  313.8 0.2 convert_reduce_fusion.1
  314.0 22.1 %all-reduce.7.cloned.1.call-done = (bf16[128,1408]{1,0:T(8,128)(2,1)}, bf16[128,1408]{1,0:T(8,128)(2,1)}) async-done(((bf16[128,1408]{1,0:T(8,128)(2,1)}, bf16[128,1408]{1,0:T(8,128)(2,1)}), (bf16[128,1408]{1,0:T(8,128)(2,1)}, bf16[128,1408]{1,0:T(8,128)(2,1)})) %all-reduce.7.cloned.1.call-update) | async-done | bytes 720912 | tf_op jit(solution)/shard_map/psum | solution.py:102
  336.1 1.2 fusion.48
  337.4 1.4 fusion.83
  338.8 0.2 multiply_reduce_fusion.3
  339.1 0.5 fusion.46
  339.6 2.0 convolution_convert_fusion
  341.6 2.5 copy.49
  344.1 0.0 all-reduce.5.cloned.1.call-start
  344.2 4.1 copy.47
  348.3 28.6 %reduce-scatter.4.cloned.1.call-done = bf16[704,704]{1,0:T(8,128)(2,1)} async-done(((bf16[1408,704]{1,0:T(8,128)(2,1)}), bf16[704,704]{1,0:T(8,128)(2,1)}) %reduce-scatter.4.cloned.1.call-update) | async-done | bytes 991248
  376.9 2.3 copy.50
  379.2 4.3 multiply_add_fusion
  383.6 5.6 %copy.48 = f32[704,1408]{1,0:T(8,128)} copy(f32[704,1408]{0,1:T(8,128)} %multiply_add_fusion) | data formatting | bytes 7929856
  389.2 49.9 %all-reduce.5.cloned.1.call-done = bf16[704,704]{1,0:T(8,128)(2,1)} async-done(((bf16[704,704]{1,0:T(8,128)(2,1)}), bf16[704,704]{1,0:T(8,128)(2,1)}) %all-reduce.5.cloned.1.call-update) | async-done | bytes 991248 | tf_op jit(solution)/shard_map/psum | solution.py:153
  439.1 2.7 convert_element_type.129
  (50 shorter events, 0.3 us)
Async XLA Ops:
  7.2 1.9 copy-start.5
  7.2 87.7 %all-gather.16.cloned.1.call-start = ((), (), s32[]{:S(2)}) async-start(), calls=%async_computation.4 | async-start | bytes 9732096 | tf_op jit(solution)/shard_map/all_gather | solution.py:15
  7.9 197.9 %all-gather.12.cloned.1.call-start = ((), (), s32[]{:S(2)}) async-start(), calls=%async_computation.1 | async-start | bytes 12976128 | tf_op jit(solution)/shard_map/all_gather | solution.py:120
  13.9 1.2 copy-start.6
  13.9 2.8 copy-start.1
  14.0 258.8 %all-gather.14.cloned.1.call-start = ((), (), s32[]{:S(2)}) async-start(), calls=%async_computation.2 | async-start | bytes 3244032 | tf_op jit(solution)/shard_map/all_gather | solution.py:136
  16.7 259.3 %all-gather.18.cloned.1.call-start = ((), (), s32[]{:S(2)}) async-start(), calls=%async_computation.5 | async-start | bytes 1622016 | tf_op jit(solution)/shard_map/all_gather | solution.py:95
  127.6 5.4 %copy-start.11 = (s32[1,128]{1,0:T(1,128)S(1)}, s32[1,128]{1,0:T(1,128)}, u32[]{:S(2)}) copy-start(s32[1,128]{1,0:T(1,128)} %param.9) | copy-start | bytes 1540
  127.6 7.3 %copy-start.9 = (f32[1408]{0:T(1024)S(1)}, f32[1408]{0:T(1024)}, u32[]{:S(2)}) copy-start(f32[1408]{0:T(1024)} %param.15) | copy-start | bytes 16900
  132.9 166.7 %all-gather.20.cloned.1.call-start = ((), (), s32[]{:S(2)}) async-start(), calls=%async_computation.6 | async-start | bytes 1622016 | tf_op jit(solution)/shard_map/all_gather | solution.py:96
  252.4 83.8 %all-reduce.7.cloned.1.call-start = ((), (), s32[]{:S(2)}) async-start(), calls=%async_computation.8 | async-start | bytes 1441792 | tf_op jit(solution)/shard_map/psum | solution.py:102
  269.7 2.6 copy-start.8
  270.5 5.5 %copy-start.7 = (bf16[1,128,704]{1,2,0:T(8,128)(2,1)S(1)}, bf16[1,128,704]{1,2,0:T(8,128)(2,1)}, u32[]{:S(2)}) copy-start(bf16[1,128,704]{1,2,0:T(8,128)(2,1)} %get-tuple-element.17) | copy-start | bytes 540676
  278.2 1.9 copy-start
  281.0 22.2 %copy-start.3 = (bf16[704,1408]{1,0:T(8,128)(2,1)S(1)}, bf16[704,1408]{1,0:T(8,128)(2,1)}, u32[]{:S(2)}) copy-start(bf16[704,1408]{1,0:T(8,128)(2,1)} %param.12) | copy-start | bytes 5947396
  299.6 5.0 %copy-start.12 = (u32[32]{0:T(128)S(1)}, u32[32]{0:T(128)}, u32[]{:S(2)}) copy-start(u32[32]{0:T(128)} %constant.55) | copy-start | bytes 388
  299.6 6.3 %copy-start.10 = (s32[1,192]{1,0:T(1,128)S(1)}, s32[1,192]{1,0:T(1,128)}, u32[]{:S(2)}) copy-start(s32[1,192]{1,0:T(1,128)} %param.10) | copy-start | bytes 2308
  304.5 72.4 %reduce-scatter.4.cloned.1.call-start = ((), (), s32[]{:S(2)}) async-start(), calls=%async_computation.7 | async-start | bytes 3244032
  336.1 2.9 copy-start.4
  344.1 35.1 %copy-start.2 = (bf16[704,1408]{0,1:T(8,128)(2,1)S(1)}, bf16[704,1408]{0,1:T(8,128)(2,1)}, u32[]{:S(2)}) copy-start(bf16[704,1408]{0,1:T(8,128)(2,1)} %all-gather.14.cloned.1.call-done) | copy-start | bytes 5947396
  344.1 95.0 %all-reduce.5.cloned.1.call-start = ((), (), s32[]{:S(2)}) async-start(), calls=%async_computation.3 | async-start | bytes 2162688 | tf_op jit(solution)/shard_map/psum | solution.py:153
Sparse Core Ops, SparseCore 0:
  9.5 85.2 all-gather.15
  96.4 109.3 all-gather.11
  207.9 33.8 all-gather.13
  243.2 28.2 all-gather.17
  273.0 26.5 all-gather.19
  304.6 31.4 all-reduce.6
  344.2 32.6 reduce-scatter.3
  379.8 59.2 all-reduce.4
